TPU v7x, 256 devices: a whole 4x4x8 slice. The times are simulated.
256 devices in a mesh: dp: 16 (over y_lo, x, core), ctx: 16 (over y_hi, z).
Axes of the slice: x: 4, y: 4 (y_hi: 2, y_lo: 2; y = y_hi * 2 + y_lo), z: 8, core: 2. Of those that a mesh axis runs over, the one named last changes fastest.
Arguments:
- roll_query: bfloat16 [16, 2048, 4096], P('dp', 'ctx'), may hold values from -12 to 12
- roll_keys: bfloat16 [16, 2048, 512], P('dp', 'ctx'), may hold values from -12 to 12
- roll_values: bfloat16 [16, 2048, 512], P('dp', 'ctx'), may hold values from -6 to 6
- pack_dest: int32 [16, 256], P(None, 'ctx'), may hold values from 0 to 15, as said below
- segment_ids: int32 [16, 2048], P('dp', 'ctx'), may hold values from 0 to 15, never falling along the last dimension, each value on 1 to 1024 neighbouring positions
- reward_bins: int32 [16, 16], P('dp'), may hold values from 0 to 511
- reward_weight: float32 [4096], replicated, may hold values from -0.5 to 0.5
Outputs:
- attention_out: bfloat16 [16, 2048, 4096], P('dp', 'ctx')
- reward_hist: float32 [512], replicated
Inputs may be any that keep to these rules, and one draw needn't show every extreme that they name: For every column j the entries pack_dest[s, j] over s are a permutation of the packed sequences. Among the 16 columns of one ctx shard, at most 1 block go from one source to one packed sequence, and exactly 1 for some pair in every shard.
All inputs are finite; a program needn't handle non-finite values.
Results may differ from a plain program's by a relative error of at most 0.004.
Values may be sent and summed in bfloat16 or wider, within the bound.
A program may use at most 64 MiB of HBM per device.

v0:
```python
import math
import jax
import jax.numpy as jnp
from jax import lax
from jax.sharding import PartitionSpec as P

HQ = 32
HK = 4
HD = 128
BLK = 8
SEGS = 16
BINS = 512
NEG = -1e30


def shifted(block, axis, distance):
    devices = range(lax.axis_size(axis))
    route = [(i - distance, i) for i in devices if i - distance in devices]
    return lax.ppermute(block, axis, route)


def block_rank(labels):
    count_all = labels.shape[0]
    earlier = jnp.arange(count_all)[:, None] < jnp.arange(count_all)[None, :]
    same_label = labels[:, None] == labels[None, :]
    return jnp.sum(jnp.where(same_label & earlier, 1, 0), axis=0).astype(jnp.int32)


def select_rows(selector, source_rows):
    flat_rows = source_rows.reshape(selector.shape[1], -1)
    return jnp.dot(selector, flat_rows, preferred_element_type=jnp.float32).astype(jnp.bfloat16)


def local(roll_query, roll_keys, roll_values, pack_dest, segment_ids, reward_bins, reward_weight):
    dp_count = lax.axis_size("dp")
    dp_self = lax.axis_index("dp")
    ctx_self = lax.axis_index("ctx")
    row_count = roll_query.shape[1]
    block_count = row_count // BLK
    q_width = roll_query.shape[2]
    kv_width = roll_keys.shape[2]
    cap_here = (block_count + dp_count - 1) // dp_count
    slot_count = dp_count * cap_here
    group_size = HQ // HK
    score_scale = 1.0 / math.sqrt(HD)
    own_dest = lax.dynamic_index_in_dim(pack_dest, dp_self, 0, keepdims=False)
    send_slot = own_dest * cap_here + block_rank(own_dest)
    send_sel = (jnp.arange(slot_count, dtype=jnp.int32)[:, None] == send_slot[None, :]).astype(
        jnp.bfloat16
    )
    send_query = select_rows(send_sel, roll_query[0]).reshape(dp_count, cap_here * BLK, q_width)
    send_keys = select_rows(send_sel, roll_keys[0]).reshape(dp_count, cap_here * BLK, kv_width)
    send_values = select_rows(send_sel, roll_values[0]).reshape(dp_count, cap_here * BLK, kv_width)
    got_query, got_keys, got_values = (
        lax.all_to_all(send_query, "dp", split_axis=0, concat_axis=0, tiled=True),
        lax.all_to_all(send_keys, "dp", split_axis=0, concat_axis=0, tiled=True),
        lax.all_to_all(send_values, "dp", split_axis=0, concat_axis=0, tiled=True),
    )
    matched = pack_dest == dp_self
    earlier = jnp.arange(block_count)[:, None] < jnp.arange(block_count)[None, :]
    recv_rank = jnp.sum(jnp.where(matched[:, :, None] & earlier[None], 1, 0), axis=1)
    source_ids = jnp.arange(dp_count, dtype=jnp.int32)[:, None]
    recv_slot = jnp.sum(jnp.where(matched, source_ids * cap_here + recv_rank, 0), axis=0)
    recv_sel = (recv_slot[:, None] == jnp.arange(slot_count, dtype=jnp.int32)[None, :]).astype(
        jnp.bfloat16
    )
    packed_query = select_rows(recv_sel, got_query).reshape(row_count, q_width)
    packed_keys = select_rows(recv_sel, got_keys).reshape(row_count, kv_width)
    packed_values = select_rows(recv_sel, got_values).reshape(row_count, kv_width)
    seg_local = segment_ids[0]
    query_heads = packed_query.reshape(row_count, HK, group_size, HD)
    query_pos = ctx_self * row_count + jnp.arange(row_count, dtype=jnp.int32)

    def attend_block(running, key_rows, value_rows, key_segments, first_row):
        key_count = key_rows.shape[0]
        key_pos = first_row + jnp.arange(key_count, dtype=jnp.int32)
        allowed = (seg_local[:, None] == key_segments[None, :]) & (
            key_pos[None, :] <= query_pos[:, None]
        )
        scores = (
            jnp.einsum(
                "qgjd,kgd->gjqk",
                query_heads,
                key_rows.reshape(key_count, HK, HD),
                preferred_element_type=jnp.float32,
            )
            * score_scale
        )
        scores = jnp.where(allowed, scores, NEG)
        run_max, run_sum, run_acc = running
        new_max = jnp.maximum(run_max, jnp.max(scores, axis=-1))
        weights = jnp.where(allowed, jnp.exp(scores - new_max[..., None]), 0.0)
        shrink = jnp.exp(run_max - new_max)
        new_sum = run_sum * shrink + jnp.sum(weights, axis=-1)
        update = jnp.einsum(
            "gjqk,kgd->qgjd",
            weights.astype(jnp.bfloat16),
            value_rows.reshape(key_count, HK, HD),
            preferred_element_type=jnp.float32,
        )
        new_acc = run_acc * jnp.transpose(shrink, (2, 0, 1))[..., None] + update
        return (new_max, new_sum, new_acc)

    initial = (
        jnp.full((HK, group_size, row_count), NEG, jnp.float32),
        jnp.zeros((HK, group_size, row_count), jnp.float32),
        jnp.zeros((row_count, HK, group_size, HD), jnp.float32),
    )
    key_rows = lax.all_gather(packed_keys, "ctx", axis=0, tiled=True)
    value_rows = lax.all_gather(packed_values, "ctx", axis=0, tiled=True)
    key_segments = lax.all_gather(seg_local, "ctx", axis=0, tiled=True)
    key_count = key_rows.shape[0]

    def sub_block(turn_index, carried):
        offset = turn_index * row_count
        return attend_block(
            carried,
            lax.dynamic_slice_in_dim(key_rows, offset, row_count, 0),
            lax.dynamic_slice_in_dim(value_rows, offset, row_count, 0),
            lax.dynamic_slice_in_dim(key_segments, offset, row_count, 0),
            offset,
        )

    final_max, final_sum, final_acc = lax.fori_loop(0, key_count // row_count, sub_block, initial)
    attended = (
        (final_acc / jnp.transpose(final_sum, (2, 0, 1))[..., None])
        .reshape(row_count, q_width)
        .astype(jnp.bfloat16)
    )
    next_first = shifted(seg_local[:1] + 1, "ctx", -1)
    next_plus = jnp.concatenate([seg_local[1:] + 1, next_first])
    is_end = next_plus != seg_local + 1
    row_reward = jnp.dot(
        attended, reward_weight, precision=lax.Precision.HIGHEST, preferred_element_type=jnp.float32
    )
    kept = jnp.where(is_end, row_reward, 0.0)
    seg_match = seg_local[:, None] == jnp.arange(SEGS, dtype=jnp.int32)[None, :]
    bin_of = jnp.sum(jnp.where(seg_match, reward_bins[0][None, :], 0), axis=1)
    bin_match = bin_of[:, None] == jnp.arange(BINS, dtype=jnp.int32)[None, :]
    local_hist = jnp.sum(jnp.where(bin_match, kept[:, None], 0.0), axis=0)
    histogram = lax.psum(local_hist, ("dp", "ctx"))
    return (attended.reshape(1, row_count, q_width), histogram)


def solution(mesh):
    in_specs = (
        P("dp", "ctx", None),
        P("dp", "ctx", None),
        P("dp", "ctx", None),
        P(None, "ctx"),
        P("dp", "ctx"),
        P("dp", None),
        P(),
    )
    out_specs = (P("dp", "ctx", None), P())
    return jax.shard_map(local, mesh=mesh, in_specs=in_specs, out_specs=out_specs, check_vma=False)
```

profile of v0, /device:TPU:1, one launch (start us, length us, event | category | flops | bytes accessed | tf_op | source)
XLA Modules:
  0.0 377.6 jit_solution(7069641416522338953)
XLA Ops:
  10.6 6.8 %all-to-all-start = ((bf16[16,8,512]{2,1,0:T(8,128)(2,1)}), bf16[16,8,512]{2,1,0:T(8,128)(2,1)S(1)}, u32[]{:S(2)}, u32[]{:S(2)}) async-start(bf16[16,8,512]{2,1,0:T(8,128)(2,1)} %bitcast.28), calls=%async_computation | async-start | bytes 262144 | tf_op jit(solution)/shard_map/all_to_all | solution.py:56
  19.0 4.5 %all-to-all-done = bf16[16,8,512]{2,1,0:T(8,128)(2,1)S(1)} async-done(((bf16[16,8,512]{2,1,0:T(8,128)(2,1)}), bf16[16,8,512]{2,1,0:T(8,128)(2,1)S(1)}, u32[]{:S(2)}, u32[]{:S(2)}) %all-to-all-start) | async-done | bytes 131104 | tf_op jit(solution)/shard_map/all_to_all | solution.py:56
  24.9 9.0 %all_to_all.15 = bf16[16,8,512]{2,1,0:T(8,128)(2,1)S(1)} all-to-all(bf16[16,8,512]{2,1,0:T(8,128)(2,1)S(1)} %bitcast.106), channel_id=1, replica_groups=mesh['dp'=16,'ctx'=16] {'dp'}, dimensions={0} | all-to-all | bytes 262144 | tf_op jit(solution)/shard_map/all_to_all | solution.py:57
  36.1 1.5 copy.33
  37.7 3.9 %all-to-all-start.1 = ((bf16[16,8,4096]{2,1,0:T(8,128)(2,1)}), bf16[16,8,4096]{2,1,0:T(8,128)(2,1)S(1)}, u32[]{:S(2)}, u32[]{:S(2)}) async-start(bf16[16,8,4096]{2,1,0:T(8,128)(2,1)} %bitcast.32), calls=%async_computation.1 | async-start | bytes 2097152 | tf_op jit(solution)/shard_map/all_to_all | solution.py:55
  41.6 1.3 collective-permute-start
  43.0 38.5 %all-gather = s32[1,2048]{1,0:T(1,128)S(1)} all-gather(s32[1,128]{1,0:T(1,128)S(1)} %copy-done.3), channel_id=2, replica_groups=mesh['dp'=16,'ctx'=16] {'ctx'}, dimensions={1}, use_global_device_ids=true | all-gather | bytes 8704 | tf_op jit(solution)/shard_map/all_gather | solution.py:111
  83.6 23.9 %all-gather.4.cloned.1.call-done = bf16[2048,512]{0,1:T(8,128)(2,1)} async-done(((bf16[128,512]{0,1:T(8,128)(2,1)}), bf16[2048,512]{0,1:T(8,128)(2,1)}) %all-gather.4.cloned.1.call-update) | async-done | bytes 2097168 | tf_op jit(solution)/shard_map/all_gather | solution.py:109
  107.5 84.1 %all-gather.6.cloned.1.call-done = bf16[2048,512]{0,1:T(8,128)(2,1)} async-done(((bf16[128,512]{0,1:T(8,128)(2,1)}), bf16[2048,512]{0,1:T(8,128)(2,1)}) %all-gather.6.cloned.1.call-update) | async-done | bytes 2097168 | tf_op jit(solution)/shard_map/all_gather | solution.py:110
  191.6 96.3 %while.18 = (s32[]{:T(128)}, f32[4,8,128]{2,1,0:T(8,128)S(1)}, f32[4,8,128]{2,1,0:T(8,128)S(1)}, f32[128,4,8,128]{0,3,2,1:T(8,128)}, s32[1,128]{1,0:T(1,128)S(1)...) while((s32[]{:T(128)}, f32[4,8,128]{2,1,0:T(8,128)S(1)}, ...), condition=%wide.region_6.7_spmd.clone, body=%wide.region_3.6_spmd.clone.sunk | while | flops 276898048 | bytes 12652751 | solution.py:124
  191.8 1.0 constant_dynamic-slice_fusion.4
  193.3 2.2 bitcast_add_fusion.3
  197.9 3.8 bitcast_add_fusion.3
  202.4 1.0 constant_dynamic-slice_fusion.4
  204.0 3.8 bitcast_add_fusion.3
  210.1 3.8 bitcast_add_fusion.3
  216.2 3.8 bitcast_add_fusion.3
  222.4 3.8 bitcast_add_fusion.3
  228.5 3.8 bitcast_add_fusion.3
  234.6 3.8 bitcast_add_fusion.3
  240.7 3.8 bitcast_add_fusion.3
  246.9 3.8 bitcast_add_fusion.3
  253.0 3.8 bitcast_add_fusion.3
  259.1 3.8 bitcast_add_fusion.3
  265.2 3.8 bitcast_add_fusion.3
  271.3 3.8 bitcast_add_fusion.3
  277.5 3.8 bitcast_add_fusion.3
  283.6 3.8 bitcast_add_fusion.3
  287.9 1.9 divide_convert_fusion
  289.8 1.3 copy.28
  291.1 1.1 compare_select_fusion
  292.4 78.4 %psum.7 = f32[512]{0:T(512)} all-reduce(f32[512]{0:T(512)S(1)} %select_reduce_fusion), channel_id=1, replica_groups=mesh['dp'=16,'ctx'=16] {'dp','ctx'}, use_global_device_ids=true, to_apply=%region_9.10 | all-reduce | flops 512 | bytes 4096 | tf_op jit(solution)/shard_map/psum | solution.py:141
  (191 shorter events, 45.4 us)
Async XLA Ops:
  7.2 284.0 %copy-start = (f32[4096]{0:T(1024)S(1)}, f32[4096]{0:T(1024)}, u32[]{:S(2)}) copy-start(f32[4096]{0:T(1024)} %param.15) | copy-start | bytes 49156
  7.2 17.5 %copy-start.2 = (bf16[1,128,512]{2,1,0:T(8,128)(2,1)S(1)}, bf16[1,128,512]{2,1,0:T(8,128)(2,1)}, u32[]{:S(2)}) copy-start(bf16[1,128,512]{2,1,0:T(8,128)(2,1)} %param.11) | copy-start | bytes 393220
  9.7 25.4 %copy-start.1 = (bf16[1,128,4096]{2,1,0:T(8,128)(2,1)S(1)}, bf16[1,128,4096]{2,1,0:T(8,128)(2,1)}, u32[]{:S(2)}) copy-start(bf16[1,128,4096]{2,1,0:T(8,128)(2,1)} %param.9) | copy-start | bytes 3145732
  10.6 12.9 %all-to-all-start = ((bf16[16,8,512]{2,1,0:T(8,128)(2,1)}), bf16[16,8,512]{2,1,0:T(8,128)(2,1)S(1)}, u32[]{:S(2)}, u32[]{:S(2)}) async-start(bf16[16,8,512]{2,1,0:T(8,128)(2,1)} %bitcast.28), calls=%async_computation | async-start | bytes 262144 | tf_op jit(solution)/shard_map/all_to_all | solution.py:56
  17.4 90.1 %all-gather.4.cloned.1.call-start = ((), (), s32[]{:S(2)}) async-start(), calls=%async_computation.3 | async-start | bytes 2228224 | tf_op jit(solution)/shard_map/all_gather | solution.py:109
  24.6 167.0 %all-gather.6.cloned.1.call-start = ((), (), s32[]{:S(2)}) async-start(), calls=%async_computation.4 | async-start | bytes 2228224 | tf_op jit(solution)/shard_map/all_gather | solution.py:110
  36.1 5.5 %copy-start.3 = (s32[1,128]{1,0:T(1,128)S(1)}, s32[1,128]{1,0:T(1,128)}, u32[]{:S(2)}) copy-start(s32[1,128]{1,0:T(1,128)} %param.13) | copy-start | bytes 1540
  36.1 45.3 %copy-start.4 = (s32[1,16]{1,0:T(1,128)S(1)}, s32[1,16]{1,0:T(1,128)}, u32[]{:S(2)}) copy-start(s32[1,16]{1,0:T(1,128)} %param.14) | copy-start | bytes 196
  37.7 43.9 %all-to-all-start.1 = ((bf16[16,8,4096]{2,1,0:T(8,128)(2,1)}), bf16[16,8,4096]{2,1,0:T(8,128)(2,1)S(1)}, u32[]{:S(2)}, u32[]{:S(2)}) async-start(bf16[16,8,4096]{2,1,0:T(8,128)(2,1)} %bitcast.32), calls=%async_computation.1 | async-start | bytes 2097152 | tf_op jit(solution)/shard_map/all_to_all | solution.py:55
  41.6 249.5 %collective-permute-start = (s32[1]{0:T(128)}, s32[1]{0:T(128)}, u32[]{:S(2)}, u32[]{:S(2)}) collective-permute-start(s32[1]{0:T(128)} %bitcast.9), channel_id=1, source_target_pairs={{1,0},{2,1},{3,2},{4,3},{5,4},{6,5},{7,6},{8,7},{9,8},{10,9},{11,1... | collective-permute-start | bytes 20 | tf_op jit(solution)/shard_map/ppermute | solution.py:19
Sparse Core Ops, SparseCore 0:
  24.7 82.7 all-gather.3
  110.0 81.5 all-gather.5
where the time goes:
time: 379 us; the launch traced here: 378 us
  blocking collectives  126 us (33%)
  waiting for transfers between devices  112 us (30%)
  matrix products  69.7 us (18%)
  local copies, waits for them, and re-layouts  26.4 us (7%)
  other arithmetic  15.5 us (4%)
  between operations  14.3 us (4%)
  starting transfers between devices  12.1 us (3%)
    all_gather x1, waiting for transfers between devices, local(): value_rows = lax.all_gather(packed_values, 'ctx', axis=0, tiled=True)  84.1 us
    psum x1, blocking collectives, local(): histogram = lax.psum(local_hist, ('dp', 'ctx'))  78.4 us
    dot_general x16, matrix products, attend_block(): jnp.einsum('gjqk,kgd->qgjd', weights.astype(jnp.bfloat16), value_rows.res...  58.6 us
    all_gather x1, blocking collectives, local(): key_segments = lax.all_gather(seg_local, 'ctx', axis=0, tiled=True)  38.5 us
    all_gather x1, waiting for transfers between devices, local(): key_rows = lax.all_gather(packed_keys, 'ctx', axis=0, tiled=True)  23.9 us
    dynamic_slice x16, local copies, waits for them, and re-layouts, sub_block(): lax.dynamic_slice_in_dim(value_rows, offset, row_count, 0)  16 us
    all_to_all x1, blocking collectives, local(): lax.all_to_all(send_values, 'dp', split_axis=0, concat_axis=0, tiled=True)  9.04 us
    reduce_sum x16, other arithmetic, attend_block(): new_sum = run_sum * shrink + jnp.sum(weights, axis=-1)  8.93 us
  transfers between devices with their start and end apart: 5, of which 3 were waited for; matrix products, arithmetic and copies ran while one was open for 28% of the time, Pallas kernels for 0%

commit v1 on v0

--- a/solution.py
+++ b/solution.py
@@ -138,7 +138,7 @@
     bin_of = jnp.sum(jnp.where(seg_match, reward_bins[0][None, :], 0), axis=1)
     bin_match = bin_of[:, None] == jnp.arange(BINS, dtype=jnp.int32)[None, :]
     local_hist = jnp.sum(jnp.where(bin_match, kept[:, None], 0.0), axis=0)
-    histogram = lax.psum(local_hist, ("dp", "ctx"))
+    histogram = jnp.sum(lax.all_gather(local_hist, ("dp", "ctx")), axis=0)
     return (attended.reshape(1, row_count, q_width), histogram)
 
 

time: 379 us -> 926 us (2.44)
  the two profiles are of different devices: /device:TPU:1 before, /device:TPU:32 now
where the time goes in v1:
time: 926 us; the launch traced here: 924 us
  blocking collectives  671 us (72%)
  waiting for transfers between devices  113 us (12%)
  matrix products  69.7 us (8%)
  local copies, waits for them, and re-layouts  26.4 us (3%)
  other arithmetic  16.5 us (2%)
  between operations  14.3 us (2%)
  starting transfers between devices  12.5 us (1%)
    all_gather x1, blocking collectives, local(): histogram = jnp.sum(lax.all_gather(local_hist, ('dp', 'ctx')), axis=0)  623 us
    all_gather x1, waiting for transfers between devices, local(): value_rows = lax.all_gather(packed_values, 'ctx', axis=0, tiled=True)  84.1 us
    dot_general x16, matrix products, attend_block(): jnp.einsum('gjqk,kgd->qgjd', weights.astype(jnp.bfloat16), value_rows.res...  58.5 us
    all_gather x1, blocking collectives, local(): key_segments = lax.all_gather(seg_local, 'ctx', axis=0, tiled=True)  39.9 us
    all_gather x1, waiting for transfers between devices, local(): key_rows = lax.all_gather(packed_keys, 'ctx', axis=0, tiled=True)  23.6 us
  transfers between devices with their start and end apart: 5, of which 3 were waited for; matrix products, arithmetic and copies ran while one was open for 11% of the time, Pallas kernels for 0%

profile of v1, /device:TPU:32, one launch (start us, length us, event | category | flops | bytes accessed | tf_op | source)
XLA Modules:
  0.0 924.5 jit_solution(3292464791563668432)
XLA Ops:
  10.6 5.4 all-to-all-start
  17.6 4.9 all-to-all-done
  23.9 9.0 all_to_all.15
  35.1 1.5 copy.39
  36.6 3.7 all-to-all-start.1
  40.3 3.3 collective-permute-start
  43.6 39.9 %all-gather = s32[1,2048]{1,0:T(1,128)S(1)} all-gather(s32[1,128]{1,0:T(1,128)S(1)} %copy-done.3), channel_id=2, replica_groups=mesh['dp'=16,'ctx'=16] {'ctx'}, dimensions={1}, use_global_device_ids=true | all-gather | bytes 8704 | tf_op jit(solution)/shard_map/all_gather | solution.py:111
  85.7 23.6 %all-gather.6.cloned.1.call-done = bf16[2048,512]{0,1:T(8,128)(2,1)} async-done(((bf16[128,512]{0,1:T(8,128)(2,1)}), bf16[2048,512]{0,1:T(8,128)(2,1)}) %all-gather.6.cloned.1.call-update) | async-done | bytes 2097168 | tf_op jit(solution)/shard_map/all_gather | solution.py:109
  109.4 84.1 %all-gather.8.cloned.1.call-done = bf16[2048,512]{0,1:T(8,128)(2,1)} async-done(((bf16[128,512]{0,1:T(8,128)(2,1)}), bf16[2048,512]{0,1:T(8,128)(2,1)}) %all-gather.8.cloned.1.call-update) | async-done | bytes 2097168 | tf_op jit(solution)/shard_map/all_gather | solution.py:110
  193.4 96.3 %while.18 = (s32[]{:T(128)}, f32[4,8,128]{2,1,0:T(8,128)S(1)}, f32[4,8,128]{2,1,0:T(8,128)S(1)}, f32[128,4,8,128]{0,3,2,1:T(8,128)}, s32[1,128]{1,0:T(1,128)S(1)...) while((s32[]{:T(128)}, f32[4,8,128]{2,1,0:T(8,128)S(1)}, ...), condition=%wide.region_6.7_spmd.clone, body=%wide.region_3.6_spmd.clone.sunk | while | flops 276898048 | bytes 12652751 | solution.py:124
  193.6 1.0 constant_dynamic-slice_fusion.4
  195.2 2.2 bitcast_add_fusion.3
  199.7 3.7 bitcast_add_fusion.3
  205.8 3.8 bitcast_add_fusion.3
  210.4 1.0 constant_dynamic-slice_fusion.4
  211.9 3.8 bitcast_add_fusion.3
  218.1 3.8 bitcast_add_fusion.3
  224.2 3.8 bitcast_add_fusion.3
  230.3 3.8 bitcast_add_fusion.3
  236.4 3.8 bitcast_add_fusion.3
  242.6 3.8 bitcast_add_fusion.3
  248.7 3.8 bitcast_add_fusion.3
  254.8 3.8 bitcast_add_fusion.3
  260.9 3.8 bitcast_add_fusion.3
  267.0 3.8 bitcast_add_fusion.3
  273.2 3.8 bitcast_add_fusion.3
  279.3 3.8 bitcast_add_fusion.3
  285.4 3.8 bitcast_add_fusion.3
  289.8 1.9 divide_convert_fusion
  291.6 1.3 copy.34
  293.0 1.1 compare_select_fusion
  294.2 622.5 %all-gather.2 = f32[256,1,512]{2,1,0:T(1,128)S(1)} all-gather(f32[1,1,512]{2,1,0:T(1,128)S(1)} %bitcast.113), channel_id=3, replica_groups=mesh['dp'=16,'ctx'=16] {'dp','ctx'}, dimensions={0}, use_global_device_ids=true | all-gather | bytes 526336 | tf_op jit(solution)/shard_map/all_gather | solution.py:141
  (192 shorter events, 46.3 us)
Async XLA Ops:
  7.2 285.8 %copy-start = (f32[4096]{0:T(1024)S(1)}, f32[4096]{0:T(1024)}, u32[]{:S(2)}) copy-start(f32[4096]{0:T(1024)} %param.15) | copy-start | bytes 49156
  7.2 16.4 %copy-start.2 = (bf16[1,128,512]{2,1,0:T(8,128)(2,1)S(1)}, bf16[1,128,512]{2,1,0:T(8,128)(2,1)}, u32[]{:S(2)}) copy-start(bf16[1,128,512]{2,1,0:T(8,128)(2,1)} %param.11) | copy-start | bytes 393220
  9.7 24.4 %copy-start.1 = (bf16[1,128,4096]{2,1,0:T(8,128)(2,1)S(1)}, bf16[1,128,4096]{2,1,0:T(8,128)(2,1)}, u32[]{:S(2)}) copy-start(bf16[1,128,4096]{2,1,0:T(8,128)(2,1)} %param.9) | copy-start | bytes 3145732
  10.6 11.9 %all-to-all-start = ((bf16[16,8,512]{2,1,0:T(8,128)(2,1)}), bf16[16,8,512]{2,1,0:T(8,128)(2,1)S(1)}, u32[]{:S(2)}, u32[]{:S(2)}) async-start(bf16[16,8,512]{2,1,0:T(8,128)(2,1)} %bitcast.29), calls=%async_computation | async-start | bytes 262144 | tf_op jit(solution)/shard_map/all_to_all | solution.py:56
  16.0 93.4 %all-gather.6.cloned.1.call-start = ((), (), s32[]{:S(2)}) async-start(), calls=%async_computation.3 | async-start | bytes 2228224 | tf_op jit(solution)/shard_map/all_gather | solution.py:109
  23.6 169.9 %all-gather.8.cloned.1.call-start = ((), (), s32[]{:S(2)}) async-start(), calls=%async_computation.4 | async-start | bytes 2228224 | tf_op jit(solution)/shard_map/all_gather | solution.py:110
  35.1 5.2 copy-start.3
  35.1 48.5 %copy-start.4 = (s32[1,16]{1,0:T(1,128)S(1)}, s32[1,16]{1,0:T(1,128)}, u32[]{:S(2)}) copy-start(s32[1,16]{1,0:T(1,128)} %param.14) | copy-start | bytes 196
  36.6 47.1 %all-to-all-start.1 = ((bf16[16,8,4096]{2,1,0:T(8,128)(2,1)}), bf16[16,8,4096]{2,1,0:T(8,128)(2,1)S(1)}, u32[]{:S(2)}, u32[]{:S(2)}) async-start(bf16[16,8,4096]{2,1,0:T(8,128)(2,1)} %bitcast.33), calls=%async_computation.1 | async-start | bytes 2097152 | tf_op jit(solution)/shard_map/all_to_all | solution.py:55
  40.3 252.6 %collective-permute-start = (s32[1]{0:T(128)}, s32[1]{0:T(128)}, u32[]{:S(2)}, u32[]{:S(2)}) collective-permute-start(s32[1]{0:T(128)} %bitcast.9), channel_id=1, source_target_pairs={{1,0},{2,1},{3,2},{4,3},{5,4},{6,5},{7,6},{8,7},{9,8},{10,9},{11,1... | collective-permute-start | bytes 20 | tf_op jit(solution)/shard_map/ppermute | solution.py:19
Sparse Core Ops, SparseCore 0:
  23.7 85.6 all-gather.5
  111.8 81.5 all-gather.7
